TPU v7x, 256 devices: a whole 4x4x8 slice. The times are simulated.
256 devices in a mesh: axial: 16 (over z, core), circ: 16 (over x, y).
Axes of the slice: x: 4, y: 4, z: 8, core: 2. Of those that a mesh axis runs over, the one named last changes fastest.
Arguments:
- right_side: float32 [128, 256, 256], P('axial', 'circ'), may hold values from -6 to 6
- stiffness: float32 [128, 256, 256], P('axial', 'circ'), may hold values from 0.03 to 0.3
- material: int32 [128, 256, 256], P('axial', 'circ'), may hold values from 0 to 15
- groups: int32 [128, 256, 256], P('axial', 'circ'), may hold values from 0 to 7, as said below
Outputs:
- solution: float32 [128, 256, 256], P('axial', 'circ')
- residual: float32 [128, 256, 256], P('axial', 'circ')
Inputs may be any that keep to these rules, and one draw needn't show every extreme that they name: `groups`: in every column of cells along the third dimension every group number from 0 to 7 occurs.
All inputs are finite; a program needn't handle non-finite values.
Results may differ from a plain program's by a relative error of at most 0.0003.
Values sent between devices are 32-bit elements; how exact they have to be, the bound alone decides.
No kernel may reach another device: no remote copies, remote signals or barrier semaphores. Data moves between devices by JAX's collectives and lax.ppermute only.
A program may use at most 128 MiB of HBM per device.

v0:
```python
import functools
import math
import jax
import jax.numpy as jnp
import numpy as np
from jax import lax
from jax.sharding import Mesh
from jax.sharding import PartitionSpec as P

LABELS = 8
CLASSES = 16
ITERS = 2
CIRC = ("circ_0", "circ_1")
AXIAL = ("axial_0", "axial_1")
AXIAL_CIRC = ("axial_0", "axial_1", "circ_0", "circ_1")
MASS_SHIFT = 0.02
PRECISE = lax.Precision.HIGHEST
HALF_STEPS = (
    (0, 0, 1),
    (0, 1, -1),
    (0, 1, 0),
    (0, 1, 1),
    (1, -1, -1),
    (1, -1, 0),
    (1, -1, 1),
    (1, 0, -1),
    (1, 0, 0),
    (1, 0, 1),
    (1, 1, -1),
    (1, 1, 0),
    (1, 1, 1),
)


def with_halo(array, sides, width, wrap):
    for axis, dim in sides:
        peers, length = (lax.axis_size(axis), array.shape[dim])
        up = [(i, (i + 1) % peers) for i in range(peers if wrap else peers - 1)]
        down = [(j, i) for i, j in up]
        last = lax.slice_in_dim(array, length - width, length, axis=dim)
        first = lax.slice_in_dim(array, 0, width, axis=dim)
        before = lax.ppermute(last, axis, up)
        after = lax.ppermute(first, axis, down)
        array = jnp.concatenate([before, array, after], axis=dim)
    return array


def copy_for_each(array, axis):
    copies = jnp.broadcast_to(array, (lax.axis_size(axis), *array.shape))
    return lax.all_to_all(copies, axis, split_axis=0, concat_axis=0, tiled=True)


def in_order(parts, dim):
    shape = list(parts.shape[1:])
    shape[dim] *= parts.shape[0]
    return jnp.moveaxis(parts, 0, dim).reshape(shape)


def collect(array, axis, dim):
    parts = copy_for_each(array, axis)
    return in_order(parts, dim)


def gather_in_order(array, axes, turns):
    parts = array[None]
    for k in turns:
        parts = lax.all_gather(parts, axes[k], axis=0, tiled=True)
    held = [lax.axis_size(axes[k]) for k in reversed(turns)]
    parts = parts.reshape(*held, *array.shape)
    turned = sorted(range(len(turns)), key=lambda place: turns[len(turns) - 1 - place])
    return parts.transpose(*turned, *range(len(turns), parts.ndim)).reshape(-1, *array.shape)


def gather_axes(array, axes, turns, dim):
    return in_order(gather_in_order(array, axes, turns), dim)


def over_axes(array, axes):
    return functools.reduce(lax.psum, axes, array)


def coefficient_table():
    rows_out = []
    for material_id in range(CLASSES):
        fiber_angle = math.pi * (material_id % 8) / 8.0
        if material_id < 8:
            fiber_dir = (math.cos(fiber_angle), math.sin(fiber_angle), 0.0)
            strength, anisotropy = (1.0, 6.0)
        else:
            fiber_dir = (0.6 * math.cos(fiber_angle), 0.6 * math.sin(fiber_angle), 0.8)
            strength, anisotropy = (0.35, 2.0)
        line_values = []
        for offset in HALF_STEPS:
            length_sq = float(offset[0] * offset[0] + offset[1] * offset[1] + offset[2] * offset[2])
            along_fiber = (
                fiber_dir[0] * offset[0] + fiber_dir[1] * offset[1] + fiber_dir[2] * offset[2]
            )
            line_values.append(
                strength * (0.15 + anisotropy * along_fiber * along_fiber / length_sq) / length_sq
            )
        rows_out.append(line_values)
    return np.array(rows_out, dtype=np.float32)


def shift_radial(values_in, amount):
    if amount == 0:
        return values_in
    blank_edge = jnp.zeros(values_in.shape[:-1] + (1,), values_in.dtype)
    if amount > 0:
        return jnp.concatenate([values_in[..., 1:], blank_edge], axis=-1)
    return jnp.concatenate([blank_edge, values_in[..., :-1]], axis=-1)


def neighbour(padded, move_axial, move_circ, move_radial):
    rows_axial = padded.shape[-3] - 2
    rows_circ = padded.shape[-2] - 2
    window = padded[
        ...,
        1 + move_axial : 1 + move_axial + rows_axial,
        1 + move_circ : 1 + move_circ + rows_circ,
        :,
    ]
    return shift_radial(window, move_radial)


def extend_field(field):
    widened = with_halo(field, ((CIRC, 1),), 1, True)
    return with_halo(widened, ((AXIAL, 0),), 1, False)


def extend_labels(labels):
    widened = with_halo(labels, ((CIRC, 2),), 1, True)
    return with_halo(widened, ((AXIAL, 1),), 1, False)


def class_onehot(labels, class_count):
    levels = jnp.arange(class_count, dtype=jnp.int32).reshape((class_count,) + (1,) * labels.ndim)
    return (labels[None] == levels).astype(jnp.float32)


def edge_weights(stiff_pad, class_pad):
    looked_up = jnp.einsum(
        "mxyr,mj->jxyr",
        class_onehot(class_pad, CLASSES),
        jnp.asarray(coefficient_table()),
        precision=PRECISE,
    )
    coefficient = stiff_pad[None] * looked_up
    weights = []
    diagonal = None
    for position, offset in enumerate(HALF_STEPS):
        centre = coefficient[position, 1:-1, 1:-1]
        forward_weight = 0.5 * (
            centre + neighbour(coefficient[position], offset[0], offset[1], offset[2])
        )
        backward_weight = 0.5 * (
            centre + neighbour(coefficient[position], -offset[0], -offset[1], -offset[2])
        )
        weights.append((forward_weight, backward_weight))
        pair_sum = forward_weight + backward_weight
        diagonal = pair_sum if diagonal is None else diagonal + pair_sum
    return (weights, MASS_SHIFT + diagonal)


def stencil_apply(padded, weights, diagonal):
    result = diagonal * padded[1:-1, 1:-1]
    for position, offset in enumerate(HALF_STEPS):
        forward_weight, backward_weight = weights[position]
        result = result - forward_weight * neighbour(padded, offset[0], offset[1], offset[2])
        result = result - backward_weight * neighbour(padded, -offset[0], -offset[1], -offset[2])
    return result


def coarse_panels(weights, diagonal, own_onehot, halo_onehot):
    stencil_terms = [((0, 0, 0), diagonal)]
    for position, offset in enumerate(HALF_STEPS):
        forward_weight, backward_weight = weights[position]
        stencil_terms.append((offset, -forward_weight))
        stencil_terms.append(((-offset[0], -offset[1], -offset[2]), -backward_weight))
    reached = None
    for offset, entry_value in stencil_terms:
        portion = shift_radial(own_onehot * entry_value[None], -offset[2])
        placed = jnp.pad(
            portion,
            ((0, 0), (1 + offset[0], 1 - offset[0]), (1 + offset[1], 1 - offset[1]), (0, 0)),
        )
        reached = placed if reached is None else reached + placed
    rows_axial = own_onehot.shape[1]
    rows_circ = own_onehot.shape[2]
    axial_parts = ((1, rows_axial + 1), (rows_axial + 1, rows_axial + 2))
    circ_parts = ((0, 1), (1, rows_circ + 1), (rows_circ + 1, rows_circ + 2))
    panel_rows = []
    for axial_start, axial_stop in axial_parts:
        panel_line = []
        for circ_start, circ_stop in circ_parts:
            panel_line.append(
                jnp.einsum(
                    "kxyr,lxyr->kl",
                    reached[:, axial_start:axial_stop, circ_start:circ_stop],
                    halo_onehot[:, axial_start:axial_stop, circ_start:circ_stop],
                    precision=PRECISE,
                )
            )
        panel_rows.append(jnp.stack(panel_line))
    return jnp.transpose(jnp.stack(panel_rows), (2, 0, 1, 3))


def cycle_blocks(panels):
    cycle_size = panels.shape[0]
    positions = jnp.arange(cycle_size, dtype=jnp.int32)
    shifts = jnp.stack(
        [
            ((positions[:, None] + offset) % cycle_size == positions[None, :]).astype(jnp.float32)
            for offset in (-1, 0, 1)
        ]
    )
    blocks = jnp.einsum("sjm,jkrsl->rjkml", shifts, panels, precision=PRECISE)
    return blocks.reshape(2, cycle_size * LABELS, cycle_size * LABELS)


def block_factor(diagonal_blocks, upper_blocks):
    block_size = diagonal_blocks.shape[1]
    identity = jnp.eye(block_size, dtype=jnp.float32)

    def advance(carried, inputs):
        inverse_prev, upper_prev = carried
        diagonal_now, upper_now = inputs
        coupling = jnp.dot(inverse_prev, upper_prev, precision=PRECISE)
        schur_block = diagonal_now - jnp.dot(coupling.T, coupling, precision=PRECISE)
        factor_now = jnp.linalg.cholesky(schur_block)
        inverse_now = lax.linalg.triangular_solve(factor_now, identity, left_side=True, lower=True)
        return ((inverse_now, upper_now), (inverse_now, coupling))

    start = (identity, jnp.zeros((block_size, block_size), jnp.float32))
    unused, (inverses, couplings) = lax.scan(advance, start, (diagonal_blocks, upper_blocks))
    return (inverses, couplings)


def coarse_solve(inverses, couplings, coarse_rhs):
    cycle_count, block_size = (inverses.shape[0], inverses.shape[1])
    parts = coarse_rhs.reshape(cycle_count, block_size)

    def forward(previous, members):
        inverse_now, coupling, part_now = members
        target = part_now - jnp.dot(coupling.T, previous, precision=PRECISE)
        solved = jnp.dot(inverse_now, target, precision=PRECISE)
        return (solved, solved)

    unused, middle = lax.scan(
        forward, jnp.zeros((block_size,), jnp.float32), (inverses, couplings, parts)
    )
    couplings_next = jnp.concatenate(
        [couplings[1:], jnp.zeros((1, block_size, block_size), jnp.float32)], axis=0
    )

    def backward(solved_next, members):
        inverse_now, coupling_next, middle_now = members
        target = middle_now - jnp.dot(coupling_next, solved_next, precision=PRECISE)
        solved = jnp.dot(inverse_now.T, target, precision=PRECISE)
        return (solved, solved)

    unused_last, solution_parts = lax.scan(
        backward,
        jnp.zeros((block_size,), jnp.float32),
        (inverses, couplings_next, middle),
        reverse=True,
    )
    return solution_parts.reshape(-1)


def spread_coarse(coarse_values, halo_onehot, axial_index, circ_index, cycle_count, cycle_size):
    by_device = coarse_values.reshape(cycle_count, cycle_size, LABELS)
    grid_rows = []
    for move_axial in (-1, 0, 1):
        target = axial_index + move_axial
        present = jnp.logical_and(target >= 0, target < cycle_count)
        cycle_row = lax.dynamic_index_in_dim(
            by_device, jnp.clip(target, 0, cycle_count - 1), 0, keepdims=False
        )
        line_values = []
        for move_circ in (-1, 0, 1):
            beside = lax.dynamic_index_in_dim(
                cycle_row, (circ_index + move_circ) % cycle_size, 0, keepdims=False
            )
            line_values.append(jnp.where(present, beside, jnp.zeros_like(beside)))
        grid_rows.append(jnp.stack(line_values))
    regional = jnp.stack(grid_rows)
    rows_axial = halo_onehot.shape[1] - 2
    rows_circ = halo_onehot.shape[2] - 2
    regional = jnp.repeat(
        regional, np.array([1, rows_axial, 1]), axis=0, total_repeat_length=rows_axial + 2
    )
    regional = jnp.repeat(
        regional, np.array([1, rows_circ, 1]), axis=1, total_repeat_length=rows_circ + 2
    )
    return jnp.einsum("lxyr,xyl->xyr", halo_onehot, regional, precision=PRECISE)


def shards(right_side, stiffness, material, groups):
    cycle_count = lax.axis_size(AXIAL)
    cycle_size = lax.axis_size(CIRC)
    axial_index = lax.axis_index(AXIAL)
    circ_index = lax.axis_index(CIRC)
    labels_pad = extend_labels(jnp.stack([material, groups]))
    weights, diagonal = edge_weights(extend_field(stiffness), labels_pad[0])
    own_onehot = class_onehot(groups, LABELS)
    halo_onehot = class_onehot(labels_pad[1], LABELS)
    panels = coarse_panels(weights, diagonal, own_onehot, halo_onehot)
    cycle_panels = collect(panels[None], CIRC, 0)
    own_cycle = cycle_blocks(cycle_panels)
    all_cycles = lax.all_gather(own_cycle[None], AXIAL, axis=0, tiled=True)
    inverses, couplings = block_factor(all_cycles[:, 0], all_cycles[:, 1])

    def project(field):
        return jnp.einsum("kxyr,xyr->k", own_onehot, field, precision=PRECISE)

    def coarse_gather(field, partial_sum):
        gathered = gather_axes(
            jnp.concatenate([project(field), partial_sum[None]])[None], AXIAL_CIRC, (0, 2, 3, 1), 0
        )
        return (gathered[:, :LABELS].reshape(-1), jnp.sum(gathered[:, LABELS]))

    def spread(coarse_rhs):
        return spread_coarse(
            coarse_solve(inverses, couplings, coarse_rhs),
            halo_onehot,
            axial_index,
            circ_index,
            cycle_count,
            cycle_size,
        )

    def deflate(residual_now):
        residual_image = stencil_apply(extend_field(residual_now), weights, diagonal)
        partial_sum = jnp.sum(residual_now * residual_now)
        coarse_rhs, norm_value = coarse_gather(residual_image, partial_sum)
        return (residual_image, norm_value, spread(coarse_rhs))

    start_rhs, unused_norm = coarse_gather(right_side, jnp.zeros((), jnp.float32))
    start_pad = spread(start_rhs)
    solution = start_pad[1:-1, 1:-1]
    residual = right_side - stencil_apply(start_pad, weights, diagonal)
    residual_image, norm_now, spread_pad = deflate(residual)
    direction = residual - spread_pad[1:-1, 1:-1]
    direction_image = None
    direction_image = residual_image - stencil_apply(spread_pad, weights, diagonal)
    for iteration in range(ITERS):
        curvature = over_axes(jnp.sum(direction * direction_image), AXIAL_CIRC)
        step_length = norm_now / curvature
        solution = solution + step_length * direction
        residual = residual - step_length * direction_image
        if iteration + 1 < ITERS:
            residual_image, norm_next, spread_pad = deflate(residual)
            beta_ratio = norm_next / norm_now
            shifted = spread_pad[1:-1, 1:-1]
            direction_image = (
                beta_ratio * direction_image
                + residual_image
                - stencil_apply(spread_pad, weights, diagonal)
            )
            direction = beta_ratio * direction + residual - shifted
            norm_now = norm_next
    return (solution, residual)


def solution(mesh):
    split = Mesh(mesh.devices.reshape(8, 2, 4, 4), ("axial_0", "axial_1", "circ_0", "circ_1"))
    placed = (
        P(AXIAL, CIRC, None),
        P(AXIAL, CIRC, None),
        P(AXIAL, CIRC, None),
        P(AXIAL, CIRC, None),
    )
    return jax.shard_map(
        shards,
        mesh=split,
        in_specs=placed,
        out_specs=(P(AXIAL, CIRC, None), P(AXIAL, CIRC, None)),
        check_vma=False,
    )
```

profile of v0, /device:TPU:10, one launch (start us, length us, event | category | flops | bytes accessed | tf_op | source)
XLA Modules:
  0.0 995.1 jit_solution(13249270050933131890)
XLA Ops:
  20.7 5.2 collective-permute-start.2
  43.5 3.6 broadcast_select_fusion.17
  47.1 5.2 broadcast_select_fusion.16
  52.3 8.7 pad_add_fusion
  69.3 12.1 %all-to-all-start = ((f32[16,1,384]{2,1,0:T(1,128)}), f32[16,1,384]{2,1,0:T(1,128)S(1)}, u32[]{:S(2)}, u32[]{:S(2)}) async-start(f32[16,1,384]{2,1,0:T(1,128)} %reshape.1223), calls=%async_computation | async-start | bytes 49152 | tf_op jit(solution)/shard_map/all_to_all | solution.py:50
  81.5 5.2 all-to-all-done
  97.4 20.7 %all-reduce.154 = f32[72]{0:T(128)S(1)} all-reduce(f32[72]{0:T(128)S(1)} %maximum_dynamic-update-slice_fusion), channel_id=2, replica_groups=mesh['axial_0'=8,'axial_1'=2,'circ_0'=4,'circ_1'=4] {'axial_0'}, use_global_device_ids=true, to_apply=%add.154 | all-reduce | flops 72 | bytes 576
  118.2 11.4 %all_gather.41 = f32[32,1,9]{2,0,1:T(8,128)S(1)} all-gather(f32[8,1,9]{2,0,1:T(8,128)S(1)} %reshape.1124), channel_id=1, replica_groups=mesh['axial_0'=8,'axial_1'=2,'circ_0'=4,'circ_1'=4] {'circ_0'}, dimensions={0}, use_global_device_ids=true | all-gather | bytes 1440 | tf_op jit(solution)/shard_map/all_gather | solution.py:67
  129.6 11.3 %all_gather.42 = f32[128,1,9]{2,0,1:T(8,128)S(1)} all-gather(f32[32,1,9]{2,0,1:T(8,128)S(1)} %all_gather.41), channel_id=1, replica_groups=mesh['axial_0'=8,'axial_1'=2,'circ_0'=4,'circ_1'=4] {'circ_1'}, dimensions={0}, use_global_device_ids=true | all-gather | bytes 5760 | tf_op jit(solution)/shard_map/all_gather | solution.py:67
  145.9 415.9 %while.113 = (s32[]{:T(128)}, f32[128,128]{1,0:T(8,128)S(1)}, f32[128,128]{1,0:T(8,128)S(1)}, f32[16,128,128]{2,1,0:T(8,128)}, f32[16,128,128]{2,1,0:T(8,128)}, ...) while((s32[]{:T(128)}, f32[128,128]{1,0:T(8,128)S(1)}, ...), condition=%wide.region_3.4_spmd.clone, body=%wide.region_0.3_spmd.clone.sunk | while | flops 75694208 | bytes 1575007 | solution.py:235
  148.3 11.7 %cholesky.75 = f32[128,128]{1,0:T(8,128)S(1)} custom-call(f32[128,128]{1,0:T(8,128)S(1)} %fusion.439), custom_call_target="Cholesky" | custom-call | tf_op jit(solution)/shard_map/while/body/eval_jaxpr/jit(cholesky)/cholesky | solution.py:230
  161.3 9.8 custom-call.22
  174.2 11.7 %cholesky.75 = f32[128,128]{1,0:T(8,128)S(1)} custom-call(f32[128,128]{1,0:T(8,128)S(1)} %fusion.439), custom_call_target="Cholesky" | custom-call | tf_op jit(solution)/shard_map/while/body/eval_jaxpr/jit(cholesky)/cholesky | solution.py:230
  187.3 9.8 custom-call.22
  200.2 11.7 %cholesky.75 = f32[128,128]{1,0:T(8,128)S(1)} custom-call(f32[128,128]{1,0:T(8,128)S(1)} %fusion.439), custom_call_target="Cholesky" | custom-call | tf_op jit(solution)/shard_map/while/body/eval_jaxpr/jit(cholesky)/cholesky | solution.py:230
  213.3 9.8 custom-call.22
  226.2 11.7 %cholesky.75 = f32[128,128]{1,0:T(8,128)S(1)} custom-call(f32[128,128]{1,0:T(8,128)S(1)} %fusion.439), custom_call_target="Cholesky" | custom-call | tf_op jit(solution)/shard_map/while/body/eval_jaxpr/jit(cholesky)/cholesky | solution.py:230
  239.2 9.8 custom-call.22
  252.2 11.7 %cholesky.75 = f32[128,128]{1,0:T(8,128)S(1)} custom-call(f32[128,128]{1,0:T(8,128)S(1)} %fusion.439), custom_call_target="Cholesky" | custom-call | tf_op jit(solution)/shard_map/while/body/eval_jaxpr/jit(cholesky)/cholesky | solution.py:230
  265.2 9.8 custom-call.22
  278.2 11.7 %cholesky.75 = f32[128,128]{1,0:T(8,128)S(1)} custom-call(f32[128,128]{1,0:T(8,128)S(1)} %fusion.439), custom_call_target="Cholesky" | custom-call | tf_op jit(solution)/shard_map/while/body/eval_jaxpr/jit(cholesky)/cholesky | solution.py:230
  291.2 9.8 custom-call.22
  304.1 11.7 %cholesky.75 = f32[128,128]{1,0:T(8,128)S(1)} custom-call(f32[128,128]{1,0:T(8,128)S(1)} %fusion.439), custom_call_target="Cholesky" | custom-call | tf_op jit(solution)/shard_map/while/body/eval_jaxpr/jit(cholesky)/cholesky | solution.py:230
  317.2 9.8 custom-call.22
  330.1 11.7 %cholesky.75 = f32[128,128]{1,0:T(8,128)S(1)} custom-call(f32[128,128]{1,0:T(8,128)S(1)} %fusion.439), custom_call_target="Cholesky" | custom-call | tf_op jit(solution)/shard_map/while/body/eval_jaxpr/jit(cholesky)/cholesky | solution.py:230
  343.2 9.8 custom-call.22
  356.1 11.7 %cholesky.75 = f32[128,128]{1,0:T(8,128)S(1)} custom-call(f32[128,128]{1,0:T(8,128)S(1)} %fusion.439), custom_call_target="Cholesky" | custom-call | tf_op jit(solution)/shard_map/while/body/eval_jaxpr/jit(cholesky)/cholesky | solution.py:230
  369.2 9.8 custom-call.22
  382.1 11.7 %cholesky.75 = f32[128,128]{1,0:T(8,128)S(1)} custom-call(f32[128,128]{1,0:T(8,128)S(1)} %fusion.439), custom_call_target="Cholesky" | custom-call | tf_op jit(solution)/shard_map/while/body/eval_jaxpr/jit(cholesky)/cholesky | solution.py:230
  395.2 9.8 custom-call.22
  408.1 11.7 %cholesky.75 = f32[128,128]{1,0:T(8,128)S(1)} custom-call(f32[128,128]{1,0:T(8,128)S(1)} %fusion.439), custom_call_target="Cholesky" | custom-call | tf_op jit(solution)/shard_map/while/body/eval_jaxpr/jit(cholesky)/cholesky | solution.py:230
  421.1 9.8 custom-call.22
  434.0 11.7 %cholesky.75 = f32[128,128]{1,0:T(8,128)S(1)} custom-call(f32[128,128]{1,0:T(8,128)S(1)} %fusion.439), custom_call_target="Cholesky" | custom-call | tf_op jit(solution)/shard_map/while/body/eval_jaxpr/jit(cholesky)/cholesky | solution.py:230
  447.1 9.8 custom-call.22
  460.0 11.7 %cholesky.75 = f32[128,128]{1,0:T(8,128)S(1)} custom-call(f32[128,128]{1,0:T(8,128)S(1)} %fusion.439), custom_call_target="Cholesky" | custom-call | tf_op jit(solution)/shard_map/while/body/eval_jaxpr/jit(cholesky)/cholesky | solution.py:230
  473.1 9.8 custom-call.22
  486.0 11.7 %cholesky.75 = f32[128,128]{1,0:T(8,128)S(1)} custom-call(f32[128,128]{1,0:T(8,128)S(1)} %fusion.439), custom_call_target="Cholesky" | custom-call | tf_op jit(solution)/shard_map/while/body/eval_jaxpr/jit(cholesky)/cholesky | solution.py:230
  499.0 9.8 custom-call.22
  512.0 11.7 %cholesky.75 = f32[128,128]{1,0:T(8,128)S(1)} custom-call(f32[128,128]{1,0:T(8,128)S(1)} %fusion.439), custom_call_target="Cholesky" | custom-call | tf_op jit(solution)/shard_map/while/body/eval_jaxpr/jit(cholesky)/cholesky | solution.py:230
  525.0 9.8 custom-call.22
  538.0 11.7 %cholesky.75 = f32[128,128]{1,0:T(8,128)S(1)} custom-call(f32[128,128]{1,0:T(8,128)S(1)} %fusion.439), custom_call_target="Cholesky" | custom-call | tf_op jit(solution)/shard_map/while/body/eval_jaxpr/jit(cholesky)/cholesky | solution.py:230
  551.0 9.8 custom-call.22
  563.0 33.8 %while.107 = (s32[]{:T(128)}, f32[128]{0:T(128)S(1)}, f32[16,128]{1,0:T(8,128)S(1)}, f32[16,128,128]{2,1,0:T(8,128)}, f32[16,128]{1,0:T(8,128)S(1)}, /*index=5*/f32[16,128,128]{2,1,0:T(8,128)}, s32[]{:T(128)}, s32[]{:T(128)}) while((s32[]{:T(128)}, f32[128]{0:T(128)S(1)}, f32[16,128]{1,0:T(8,128)S(1)}, f32[16,128,128]{2,1,0:T(8,128)}, ...), condition=%wide.region_5.6_spmd, body=%wide.region_4.5_spmd.sunk | while | flops 393346 | bytes 136281 | solution.py:249
  596.9 20.4 %while.108 = (s32[]{:T(128)}, f32[128]{0:T(128)S(1)}, f32[16,128]{1,0:T(8,128)S(1)}, f32[16,128,128]{2,1,0:T(8,128)}, f32[16,128]{1,0:T(8,128)S(1)}, /*index=5*/...) while((s32[]{:T(128)}, f32[128]{0:T(128)S(1)}, f32[16,128]{1,0:T(8,128)S(1)}, ...), condition=%wide.region_7.8_spmd, body=%wide.region_6.7_spmd.sunk | while | flops 393347 | bytes 135793 | solution.py:262
  631.0 3.3 collective-permute-start.11
  639.0 18.2 %all-reduce.155 = f32[72]{0:T(128)S(1)} all-reduce(f32[72]{0:T(128)S(1)} %maximum_dynamic-update-slice_fusion.1), channel_id=3, replica_groups=mesh['axial_0'=8,'axial_1'=2,'circ_0'=4,'circ_1'=4] {'axial_0'}, use_global_device_ids=true, to_apply=%add.155 | all-reduce | flops 72 | bytes 576
  657.4 11.3 %all_gather.45 = f32[32,1,9]{2,0,1:T(8,128)S(1)} all-gather(f32[8,1,9]{2,0,1:T(8,128)S(1)} %reshape.1125), channel_id=1, replica_groups=mesh['axial_0'=8,'axial_1'=2,'circ_0'=4,'circ_1'=4] {'circ_0'}, dimensions={0}, use_global_device_ids=true | all-gather | bytes 1440 | tf_op jit(solution)/shard_map/all_gather | solution.py:67
  668.7 13.1 %all_gather.46 = f32[128,1,9]{2,0,1:T(8,128)S(1)} all-gather(f32[32,1,9]{2,0,1:T(8,128)S(1)} %all_gather.45), channel_id=1, replica_groups=mesh['axial_0'=8,'axial_1'=2,'circ_0'=4,'circ_1'=4] {'circ_1'}, dimensions={0}, use_global_device_ids=true | all-gather | bytes 5760 | tf_op jit(solution)/shard_map/all_gather | solution.py:67
  683.9 33.7 %while.109 = (s32[]{:T(128)}, f32[128]{0:T(128)S(1)}, f32[16,128]{1,0:T(8,128)S(1)}, f32[16,128,128]{2,1,0:T(8,128)}, f32[16,128]{1,0:T(8,128)S(1)}, /*index=5*/f32[16,128,128]{2,1,0:T(8,128)}, s32[]{:T(128)}, s32[]{:T(128)}) while((s32[]{:T(128)}, f32[128]{0:T(128)S(1)}, f32[16,128]{1,0:T(8,128)S(1)}, f32[16,128,128]{2,1,0:T(8,128)}, ...), condition=%wide.region_17.20_spmd, body=%wide.region_16.19_spmd.sunk | while | flops 393346 | bytes 136281 | solution.py:249
  717.7 33.8 %while.110 = (s32[]{:T(128)}, f32[128]{0:T(128)S(1)}, f32[16,128]{1,0:T(8,128)S(1)}, f32[16,128,128]{2,1,0:T(8,128)}, f32[16,128]{1,0:T(8,128)S(1)}, /*index=5*/...) while((s32[]{:T(128)}, f32[128]{0:T(128)S(1)}, f32[16,128]{1,0:T(8,128)S(1)}, ...), condition=%wide.region_19.22_spmd, body=%wide.region_18.21_spmd.sunk | while | flops 393347 | bytes 135793 | solution.py:262
  758.6 16.6 %psum.56 = f32[]{:T(128)} all-reduce(f32[]{:T(128)} %get-tuple-element.743), channel_id=1, replica_groups=mesh['axial_0'=8,'axial_1'=2,'circ_0'=4,'circ_1'=4] {'axial_0'}, use_global_device_ids=true, to_apply=%region_27.30 | all-reduce | flops 1 | bytes 8 | tf_op jit(solution)/shard_map/psum | solution.py:79
  775.2 3.1 psum.57
  778.3 10.8 %psum.58 = f32[]{:T(128)} all-reduce(f32[]{:T(128)} %psum.57), channel_id=1, replica_groups=mesh['axial_0'=8,'axial_1'=2,'circ_0'=4,'circ_1'=4] {'circ_0'}, use_global_device_ids=true, to_apply=%region_29.32 | all-reduce | flops 1 | bytes 8 | tf_op jit(solution)/shard_map/psum | solution.py:79
  790.7 11.6 %psum.59 = f32[]{:T(128)} all-reduce(f32[]{:T(128)} %psum.58), channel_id=1, replica_groups=mesh['axial_0'=8,'axial_1'=2,'circ_0'=4,'circ_1'=4] {'circ_1'}, use_global_device_ids=true, to_apply=%region_30.33 | all-reduce | flops 1 | bytes 8 | tf_op jit(solution)/shard_map/psum | solution.py:79
  818.5 16.5 %all-reduce.156 = f32[72]{0:T(128)S(1)} all-reduce(f32[72]{0:T(128)S(1)} %maximum_dynamic-update-slice_fusion.2), channel_id=4, replica_groups=mesh['axial_0'=8,'axial_1'=2,'circ_0'=4,'circ_1'=4] {'axial_0'}, use_global_device_ids=true, to_apply=%add.156 | all-reduce | flops 72 | bytes 576
  835.1 10.8 %all_gather.49 = f32[32,1,9]{2,0,1:T(8,128)S(1)} all-gather(f32[8,1,9]{2,0,1:T(8,128)S(1)} %reshape.1126), channel_id=1, replica_groups=mesh['axial_0'=8,'axial_1'=2,'circ_0'=4,'circ_1'=4] {'circ_0'}, dimensions={0}, use_global_device_ids=true | all-gather | bytes 1440 | tf_op jit(solution)/shard_map/all_gather | solution.py:67
  845.9 13.9 %all_gather.50 = f32[128,1,9]{2,0,1:T(8,128)S(1)} all-gather(f32[32,1,9]{2,0,1:T(8,128)S(1)} %all_gather.49), channel_id=1, replica_groups=mesh['axial_0'=8,'axial_1'=2,'circ_0'=4,'circ_1'=4] {'circ_1'}, dimensions={0}, use_global_device_ids=true | all-gather | bytes 5760 | tf_op jit(solution)/shard_map/all_gather | solution.py:67
  862.9 33.8 %while.111 = (s32[]{:T(128)}, f32[128]{0:T(128)S(1)}, f32[16,128]{1,0:T(8,128)S(1)}, f32[16,128,128]{2,1,0:T(8,128)}, f32[16,128]{1,0:T(8,128)S(1)}, /*index=5*/f32[16,128,128]{2,1,0:T(8,128)}, s32[]{:T(128)}, s32[]{:T(128)}) while((s32[]{:T(128)}, f32[128]{0:T(128)S(1)}, f32[16,128]{1,0:T(8,128)S(1)}, f32[16,128,128]{2,1,0:T(8,128)}, ...), condition=%wide.region_34.37_spmd, body=%wide.region_33.36_spmd.sunk | while | flops 393346 | bytes 136281 | solution.py:249
  896.7 33.8 %while.112 = (s32[]{:T(128)}, f32[128]{0:T(128)S(1)}, f32[16,128]{1,0:T(8,128)S(1)}, f32[16,128,128]{2,1,0:T(8,128)}, f32[16,128]{1,0:T(8,128)S(1)}, /*index=5*/...) while((s32[]{:T(128)}, f32[128]{0:T(128)S(1)}, f32[16,128]{1,0:T(8,128)S(1)}, ...), condition=%wide.region_36.39_spmd, body=%wide.region_35.38_spmd.sunk | while | flops 393347 | bytes 135793 | solution.py:262
  937.4 4.1 multiply_reduce_fusion
  941.5 17.5 %psum.60 = f32[]{:T(128)} all-reduce(f32[]{:T(128)} %get-tuple-element.739), channel_id=1, replica_groups=mesh['axial_0'=8,'axial_1'=2,'circ_0'=4,'circ_1'=4] {'axial_0'}, use_global_device_ids=true, to_apply=%region_44.47 | all-reduce | flops 1 | bytes 8 | tf_op jit(solution)/shard_map/psum | solution.py:79
  959.1 3.1 psum.61
  962.1 11.0 %psum.62 = f32[]{:T(128)} all-reduce(f32[]{:T(128)} %psum.61), channel_id=1, replica_groups=mesh['axial_0'=8,'axial_1'=2,'circ_0'=4,'circ_1'=4] {'circ_0'}, use_global_device_ids=true, to_apply=%region_46.49 | all-reduce | flops 1 | bytes 8 | tf_op jit(solution)/shard_map/psum | solution.py:79
  973.2 11.6 %psum.63 = f32[]{:T(128)} all-reduce(f32[]{:T(128)} %psum.62), channel_id=1, replica_groups=mesh['axial_0'=8,'axial_1'=2,'circ_0'=4,'circ_1'=4] {'circ_1'}, use_global_device_ids=true, to_apply=%region_47.50 | all-reduce | flops 1 | bytes 8 | tf_op jit(solution)/shard_map/psum | solution.py:79
  (835 shorter events, 366.3 us)
Async XLA Ops:
  7.2 23.1 %copy-start.48 = (s32[8,16,256]{2,1,0:T(8,128)S(1)}, s32[8,16,256]{2,1,0:T(8,128)}, u32[]{:S(2)}) copy-start(s32[8,16,256]{2,1,0:T(8,128)} %param.43) | copy-start | bytes 393220
  7.2 23.1 %copy-start.47 = (s32[8,16,256]{2,1,0:T(8,128)S(1)}, s32[8,16,256]{2,1,0:T(8,128)}, u32[]{:S(2)}) copy-start(s32[8,16,256]{2,1,0:T(8,128)} %param.44) | copy-start | bytes 393220
  7.2 20.5 %copy-start.50 = (f32[8,16,256]{2,1,0:T(8,128)S(1)}, f32[8,16,256]{2,1,0:T(8,128)}, u32[]{:S(2)}) copy-start(f32[8,16,256]{2,1,0:T(8,128)} %param.42) | copy-start | bytes 393220
  8.2 11.6 %collective-permute-start = (s32[2,8,1,256]{3,2,1,0:T(1,128)S(1)}, s32[2,8,1,256]{3,2,1,0:T(1,128)S(1)}, u32[]{:S(2)}, u32[]{:S(2)}) collective-permute-start(s32[2,8,1,256]{3,2,1,0:T(1,128)S(1)} %get-tuple-element.828), channel_id=1, source_target_pairs={{0,1},{1,2},{2,3},{3,4},{4,5},{5,6},{6,7},{7,8},{8,9},{9,10},{10,1... | collective-permute-start | bytes 49160 | tf_op jit(solution)/shard_map/ppermute | solution.py:42
  9.9 10.0 %collective-permute-start.1 = (s32[2,8,1,256]{3,2,1,0:T(1,128)S(1)}, s32[2,8,1,256]{3,2,1,0:T(1,128)S(1)}, u32[]{:S(2)}, u32[]{:S(2)}) collective-permute-start(s32[2,8,1,256]{3,2,1,0:T(1,128)S(1)} %get-tuple-element.829), channel_id=1, source_target_pairs={{1,0},{2,1},{3,2},{4,3},{5,4},{6,5},{7,6},{8,7},{9,8},{10,9},{11,1... | collective-permute-start | bytes 49160 | tf_op jit(solution)/shard_map/ppermute | solution.py:43
  11.2 4.3 collective-permute-start.4
  12.9 3.7 collective-permute-start.5
  15.1 32.0 %copy-start.44 = (pred[8,8,16,256]{3,0,1,2:T(8,128)(4,1)}, pred[8,8,16,256]{3,0,1,2:T(8,128)(4,1)S(1)}, u32[]{:S(2)}) copy-start(pred[8,8,16,256]{3,0,1,2:T(8,128)(4,1)S(1)} %iota_compare_fusion.6) | copy-start | bytes 786436
  15.1 15.2 %copy-start.56 = (f32[16,13,1,1]{0,1,3,2:T(8,128)S(1)}, f32[16,13,1,1]{0,1,3,2:T(8,128)}, u32[]{:S(2)}) copy-start(f32[16,13,1,1]{0,1,3,2:T(8,128)} %constant.1468) | copy-start | bytes 2500
  17.3 10.4 %collective-permute-start.6 = (f32[1,18,256]{2,1,0:T(8,128)S(1)}, f32[1,18,256]{2,1,0:T(8,128)S(1)}, u32[]{:S(2)}, u32[]{:S(2)}) collective-permute-start(f32[1,18,256]{2,1,0:T(8,128)S(1)} %get-tuple-element.934), channel_id=1, source_target_pairs={{0,16},{16,32},{32,48},{48,64},{64,80},{80,96},{96,112},{112,128},... | collective-permute-start | bytes 55304 | tf_op jit(solution)/shard_map/ppermute | solution.py:42
  18.6 9.1 collective-permute-start.7
  20.7 7.1 collective-permute-start.2
  25.9 4.4 collective-permute-start.3
  37.1 1.1 copy-start.33
  37.1 1.2 copy-start.28
  37.1 1.4 copy-start.16
  37.1 1.5 copy-start.10
  37.1 1.6 copy-start.8
  37.1 1.7 copy-start.2
  37.1 1.9 copy-start
  37.1 2.0 copy-start.18
  37.1 2.1 copy-start.38
  37.2 2.3 copy-start.23
  37.2 2.5 copy-start.20
  37.2 2.7 copy-start.14
  37.2 2.9 copy-start.12
  37.2 3.1 copy-start.6
  37.2 3.3 copy-start.4
  69.3 17.5 %all-to-all-start = ((f32[16,1,384]{2,1,0:T(1,128)}), f32[16,1,384]{2,1,0:T(1,128)S(1)}, u32[]{:S(2)}, u32[]{:S(2)}) async-start(f32[16,1,384]{2,1,0:T(1,128)} %reshape.1223), calls=%async_computation | async-start | bytes 49152 | tf_op jit(solution)/shard_map/all_to_all | solution.py:50
  81.4 61.7 %all-gather.5.cloned.1.call-start = ((), (), s32[]{:S(2)}) async-start(), calls=%async_computation.1 | async-start | bytes 2228224 | tf_op jit(solution)/shard_map/all_gather | solution.py:311
  92.0 1.7 copy-start.59
  93.7 49.4 %copy-start.58 = (s32[10]{0:T(128)S(1)}, s32[10]{0:T(128)}, u32[]{:S(2)}) copy-start(s32[10]{0:T(128)} %constant.1462) | copy-start | bytes 124
  93.7 49.4 %copy-start.57 = (s32[18]{0:T(128)S(1)}, s32[18]{0:T(128)}, u32[]{:S(2)}) copy-start(s32[18]{0:T(128)} %constant.1463) | copy-start | bytes 220
  596.9 22.3 %copy-start.54 = (pred[8,10,18,256]{3,0,1,2:T(8,128)(4,1)S(1)}, pred[8,10,18,256]{3,0,1,2:T(8,128)(4,1)}, u32[]{:S(2)}) copy-start(pred[8,10,18,256]{3,0,1,2:T(8,128)(4,1)} %iota_compare_fusion.5) | copy-start | bytes 1105924
  617.3 1.9 copy-start.43
  620.2 1.1 copy-start.7
  620.2 1.1 copy-start.9
  620.2 1.2 copy-start.11
  620.2 1.2 copy-start.13
  620.2 1.2 copy-start.15
  620.2 1.3 copy-start.17
  620.2 1.3 copy-start.19
  620.2 1.3 copy-start.21
  620.2 1.4 copy-start.24
  620.2 1.4 copy-start.29
  620.3 1.4 copy-start.34
  620.3 1.4 copy-start.39
  620.3 1.5 copy-start.55
  623.2 3.7 collective-permute-start.8
  625.3 4.3 collective-permute-start.9
  629.7 4.7 collective-permute-start.10
  631.0 3.9 collective-permute-start.11
  634.9 1.1 copy-start.40
  637.1 1.2 copy-start.52
  683.8 68.2 %copy-start.49 = (f32[2,4,4,8,1,9]{5,1,2,0,3,4:T(4,128)}, f32[2,4,4,8,1,9]{5,1,2,0,3,4:T(4,128)S(1)}, u32[]{:S(2)}) copy-start(f32[2,4,4,8,1,9]{5,1,2,0,3,4:T(4,128)S(1)} %copy.274) | copy-start | bytes 27652
  755.3 1.1 copy-start.41
  755.3 1.1 copy-start.53
  805.3 3.7 collective-permute-start.12
  805.4 3.7 collective-permute-start.13
  809.1 4.5 collective-permute-start.14
  810.4 3.9 collective-permute-start.15
  814.4 1.1 copy-start.37
  814.4 1.1 copy-start.42
  816.5 1.2 copy-start.51
  (14 other events, 13.6 us)
Sparse Core Ops, SparseCore 0:
  93.8 43.4 all-gather.4
where the time goes:
time: 1010 us; the launch traced here: 995 us
  other arithmetic  409 us (40%)
  matrix products  235 us (23%)
  blocking collectives  218 us (22%)
  local copies, waits for them, and re-layouts  51.7 us (5%)
  starting transfers between devices  39.7 us (4%)
  between operations  21.3 us (2%)
  waiting for transfers between devices  16 us (2%)
    another operation x48, other arithmetic, advance(): factor_now = jnp.linalg.cholesky(schur_block)  198 us
    another operation x32, other arithmetic, advance(): lax.linalg.triangular_solve(factor_now, identity, left_side=True, lower=T...  167 us
    psum x8, blocking collectives, over_axes(): return functools.reduce(lax.psum, axes, array)  85.2 us
    all_gather x9, blocking collectives, gather_in_order(): parts = lax.all_gather(parts, axes[k], axis=0, tiled=True)  77.8 us
    unnamed x3, blocking collectives  55.5 us
    dot_general x48, matrix products, backward(): solved = jnp.dot(inverse_now.T, target, precision=PRECISE)  49.9 us
    dot_general x48, matrix products, forward(): solved = jnp.dot(inverse_now, target, precision=PRECISE)  49.3 us
    dot_general x48, matrix products, forward(): target = part_now - jnp.dot(coupling.T, previous, precision=PRECISE)  48.1 us
  transfers between devices with their start and end apart: 18, of which 10 were waited for; matrix products, arithmetic and copies ran while one was open for 1% of the time, Pallas kernels for 0%

commit v1 on v0

--- a/solution.py
+++ b/solution.py
@@ -64,7 +64,9 @@
 def gather_in_order(array, axes, turns):
     parts = array[None]
     for k in turns:
-        parts = lax.all_gather(parts, axes[k], axis=0, tiled=True)
+        parts = jnp.concatenate(
+            lax.all_to_all(jnp.stack([parts] * lax.axis_size(axes[k])), axes[k], 0, 0), axis=0
+        )
     held = [lax.axis_size(axes[k]) for k in reversed(turns)]
     parts = parts.reshape(*held, *array.shape)
     turned = sorted(range(len(turns)), key=lambda place: turns[len(turns) - 1 - place])

time: 1010 us -> 993 us (0.983)
  blocking collectives: 218 us -> 131 us
  starting transfers between devices: 39.7 us -> 76.6 us
  waiting for transfers between devices: 16 us -> 39 us
    all_gather x9 -> x0, blocking collectives: 77.8 us -> none  [gather_in_order(): parts = lax.all_gather(parts, axes[k], axis=0, tiled=True)]
    unnamed x3 -> x0, blocking collectives: 55.5 us -> none
    all_to_all x0 -> x7, blocking collectives: none -> 55.2 us  [gather_in_order(): lax.all_to_all(jnp.stack([parts] * lax.axis_size(axes[k])), axes[k], 0, 0)]
    all_to_all x0 -> x5, starting transfers between devices: none -> 36.9 us  [gather_in_order(): lax.all_to_all(jnp.stack([parts] * lax.axis_size(axes[k])), axes[k], 0, 0)]
    all_to_all x0 -> x5, waiting for transfers between devices: none -> 23.1 us  [gather_in_order(): lax.all_to_all(jnp.stack([parts] * lax.axis_size(axes[k])), axes[k], 0, 0)]
  transfers between devices with their start and end apart: 18 -> 23, of which waited for: 10 -> 15; matrix products, arithmetic and copies ran while one was open for 1% -> 1% of each run, Pallas kernels for 0% -> 0%
where the time goes in v1:
time: 993 us; the launch traced here: 978 us
  other arithmetic  414 us (42%)
  matrix products  235 us (24%)
  blocking collectives  131 us (13%)
  starting transfers between devices  76.6 us (8%)
  local copies, waits for them, and re-layouts  58.6 us (6%)
  waiting for transfers between devices  39 us (4%)
  between operations  20.6 us (2%)
    another operation x48, other arithmetic, advance(): factor_now = jnp.linalg.cholesky(schur_block)  198 us
    another operation x32, other arithmetic, advance(): lax.linalg.triangular_solve(factor_now, identity, left_side=True, lower=T...  167 us
    psum x8, blocking collectives, over_axes(): return functools.reduce(lax.psum, axes, array)  76.1 us
    all_to_all x7, blocking collectives, gather_in_order(): lax.all_to_all(jnp.stack([parts] * lax.axis_size(axes[k])), axes[k], 0, 0)  55.2 us
    dot_general x48, matrix products, backward(): solved = jnp.dot(inverse_now.T, target, precision=PRECISE)  49.9 us
    dot_general x48, matrix products, forward(): solved = jnp.dot(inverse_now, target, precision=PRECISE)  49.3 us
    dot_general x48, matrix products, forward(): target = part_now - jnp.dot(coupling.T, previous, precision=PRECISE)  48.1 us
    all_to_all x5, starting transfers between devices, gather_in_order(): lax.all_to_all(jnp.stack([parts] * lax.axis_size(axes[k])), axes[k], 0, 0)  36.9 us
  transfers between devices with their start and end apart: 23, of which 15 were waited for; matrix products, arithmetic and copies ran while one was open for 1% of the time, Pallas kernels for 0%

profile of v1, /device:TPU:10, one launch (start us, length us, event | category | flops | bytes accessed | tf_op | source)
XLA Modules:
  0.0 978.2 jit_solution(3313607496544461670)
XLA Ops:
  20.7 5.2 collective-permute-start.2
  47.0 5.3 broadcast_select_fusion.16
  52.3 8.7 pad_add_fusion
  69.3 12.1 %all-to-all-start = ((f32[16,1,384]{2,1,0:T(1,128)}), f32[16,1,384]{2,1,0:T(1,128)S(1)}, u32[]{:S(2)}, u32[]{:S(2)}) async-start(f32[16,1,384]{2,1,0:T(1,128)} %reshape.1223), calls=%async_computation | async-start | bytes 49152 | tf_op jit(solution)/shard_map/all_to_all | solution.py:50
  81.5 5.2 all-to-all-done
  96.6 11.6 %all-to-all-start.1 = ((f32[8,1,1,9]{3,2,1,0:T(1,128)}), f32[8,1,1,9]{3,2,1,0:T(1,128)S(1)}, u32[]{:S(2)}, u32[]{:S(2)}) async-start(f32[8,1,1,9]{3,2,1,0:T(1,128)} %stack.193), calls=%async_computation.1 | async-start | bytes 8192 | tf_op jit(solution)/shard_map/all_to_all | solution.py:68
  108.3 7.7 all-to-all-done.1
  116.6 4.7 all-to-all-start.2
  121.2 3.9 all-to-all-done.2
  126.6 4.7 all-to-all-start.3
  131.3 3.9 all-to-all-done.3
  143.1 415.6 %while.113 = (s32[]{:T(128)}, f32[128,128]{1,0:T(8,128)S(1)}, f32[128,128]{1,0:T(8,128)S(1)}, f32[16,128,128]{2,1,0:T(8,128)}, f32[16,128,128]{2,1,0:T(8,128)}, ...) while((s32[]{:T(128)}, f32[128,128]{1,0:T(8,128)S(1)}, ...), condition=%wide.region_3.4_spmd.clone, body=%wide.region_0.3_spmd.clone.sunk | while | flops 75694208 | bytes 1575007 | solution.py:237
  145.5 11.7 %cholesky.75 = f32[128,128]{1,0:T(8,128)S(1)} custom-call(f32[128,128]{1,0:T(8,128)S(1)} %fusion.439), custom_call_target="Cholesky" | custom-call | tf_op jit(solution)/shard_map/while/body/eval_jaxpr/jit(cholesky)/cholesky | solution.py:232
  158.6 9.8 %custom-call.22 = f32[1,128,128]{1,2,0:T(8,128)S(1)} custom-call(f32[1,128,128]{2,1,0:T(8,128)S(1)} %fusion.440), custom_call_target="InvertDiagBlocksLowerTriangular" | custom-call | tf_op jit(solution)/shard_map/while/body/eval_jaxpr/triangular_solve | solution.py:233
  171.5 11.7 %cholesky.75 = f32[128,128]{1,0:T(8,128)S(1)} custom-call(f32[128,128]{1,0:T(8,128)S(1)} %fusion.439), custom_call_target="Cholesky" | custom-call | tf_op jit(solution)/shard_map/while/body/eval_jaxpr/jit(cholesky)/cholesky | solution.py:232
  184.5 9.8 %custom-call.22 = f32[1,128,128]{1,2,0:T(8,128)S(1)} custom-call(f32[1,128,128]{2,1,0:T(8,128)S(1)} %fusion.440), custom_call_target="InvertDiagBlocksLowerTriangular" | custom-call | tf_op jit(solution)/shard_map/while/body/eval_jaxpr/triangular_solve | solution.py:233
  197.4 11.7 %cholesky.75 = f32[128,128]{1,0:T(8,128)S(1)} custom-call(f32[128,128]{1,0:T(8,128)S(1)} %fusion.439), custom_call_target="Cholesky" | custom-call | tf_op jit(solution)/shard_map/while/body/eval_jaxpr/jit(cholesky)/cholesky | solution.py:232
  210.5 9.8 %custom-call.22 = f32[1,128,128]{1,2,0:T(8,128)S(1)} custom-call(f32[1,128,128]{2,1,0:T(8,128)S(1)} %fusion.440), custom_call_target="InvertDiagBlocksLowerTriangular" | custom-call | tf_op jit(solution)/shard_map/while/body/eval_jaxpr/triangular_solve | solution.py:233
  223.4 11.7 %cholesky.75 = f32[128,128]{1,0:T(8,128)S(1)} custom-call(f32[128,128]{1,0:T(8,128)S(1)} %fusion.439), custom_call_target="Cholesky" | custom-call | tf_op jit(solution)/shard_map/while/body/eval_jaxpr/jit(cholesky)/cholesky | solution.py:232
  236.5 9.8 %custom-call.22 = f32[1,128,128]{1,2,0:T(8,128)S(1)} custom-call(f32[1,128,128]{2,1,0:T(8,128)S(1)} %fusion.440), custom_call_target="InvertDiagBlocksLowerTriangular" | custom-call | tf_op jit(solution)/shard_map/while/body/eval_jaxpr/triangular_solve | solution.py:233
  249.4 11.7 %cholesky.75 = f32[128,128]{1,0:T(8,128)S(1)} custom-call(f32[128,128]{1,0:T(8,128)S(1)} %fusion.439), custom_call_target="Cholesky" | custom-call | tf_op jit(solution)/shard_map/while/body/eval_jaxpr/jit(cholesky)/cholesky | solution.py:232
  262.4 9.8 %custom-call.22 = f32[1,128,128]{1,2,0:T(8,128)S(1)} custom-call(f32[1,128,128]{2,1,0:T(8,128)S(1)} %fusion.440), custom_call_target="InvertDiagBlocksLowerTriangular" | custom-call | tf_op jit(solution)/shard_map/while/body/eval_jaxpr/triangular_solve | solution.py:233
  275.3 11.7 %cholesky.75 = f32[128,128]{1,0:T(8,128)S(1)} custom-call(f32[128,128]{1,0:T(8,128)S(1)} %fusion.439), custom_call_target="Cholesky" | custom-call | tf_op jit(solution)/shard_map/while/body/eval_jaxpr/jit(cholesky)/cholesky | solution.py:232
  288.4 9.8 %custom-call.22 = f32[1,128,128]{1,2,0:T(8,128)S(1)} custom-call(f32[1,128,128]{2,1,0:T(8,128)S(1)} %fusion.440), custom_call_target="InvertDiagBlocksLowerTriangular" | custom-call | tf_op jit(solution)/shard_map/while/body/eval_jaxpr/triangular_solve | solution.py:233
  301.3 11.7 %cholesky.75 = f32[128,128]{1,0:T(8,128)S(1)} custom-call(f32[128,128]{1,0:T(8,128)S(1)} %fusion.439), custom_call_target="Cholesky" | custom-call | tf_op jit(solution)/shard_map/while/body/eval_jaxpr/jit(cholesky)/cholesky | solution.py:232
  314.4 9.8 %custom-call.22 = f32[1,128,128]{1,2,0:T(8,128)S(1)} custom-call(f32[1,128,128]{2,1,0:T(8,128)S(1)} %fusion.440), custom_call_target="InvertDiagBlocksLowerTriangular" | custom-call | tf_op jit(solution)/shard_map/while/body/eval_jaxpr/triangular_solve | solution.py:233
  327.3 11.7 %cholesky.75 = f32[128,128]{1,0:T(8,128)S(1)} custom-call(f32[128,128]{1,0:T(8,128)S(1)} %fusion.439), custom_call_target="Cholesky" | custom-call | tf_op jit(solution)/shard_map/while/body/eval_jaxpr/jit(cholesky)/cholesky | solution.py:232
  340.3 9.8 %custom-call.22 = f32[1,128,128]{1,2,0:T(8,128)S(1)} custom-call(f32[1,128,128]{2,1,0:T(8,128)S(1)} %fusion.440), custom_call_target="InvertDiagBlocksLowerTriangular" | custom-call | tf_op jit(solution)/shard_map/while/body/eval_jaxpr/triangular_solve | solution.py:233
  353.2 11.7 %cholesky.75 = f32[128,128]{1,0:T(8,128)S(1)} custom-call(f32[128,128]{1,0:T(8,128)S(1)} %fusion.439), custom_call_target="Cholesky" | custom-call | tf_op jit(solution)/shard_map/while/body/eval_jaxpr/jit(cholesky)/cholesky | solution.py:232
  366.3 9.8 %custom-call.22 = f32[1,128,128]{1,2,0:T(8,128)S(1)} custom-call(f32[1,128,128]{2,1,0:T(8,128)S(1)} %fusion.440), custom_call_target="InvertDiagBlocksLowerTriangular" | custom-call | tf_op jit(solution)/shard_map/while/body/eval_jaxpr/triangular_solve | solution.py:233
  379.2 11.7 %cholesky.75 = f32[128,128]{1,0:T(8,128)S(1)} custom-call(f32[128,128]{1,0:T(8,128)S(1)} %fusion.439), custom_call_target="Cholesky" | custom-call | tf_op jit(solution)/shard_map/while/body/eval_jaxpr/jit(cholesky)/cholesky | solution.py:232
  392.2 9.8 %custom-call.22 = f32[1,128,128]{1,2,0:T(8,128)S(1)} custom-call(f32[1,128,128]{2,1,0:T(8,128)S(1)} %fusion.440), custom_call_target="InvertDiagBlocksLowerTriangular" | custom-call | tf_op jit(solution)/shard_map/while/body/eval_jaxpr/triangular_solve | solution.py:233
  405.1 11.7 %cholesky.75 = f32[128,128]{1,0:T(8,128)S(1)} custom-call(f32[128,128]{1,0:T(8,128)S(1)} %fusion.439), custom_call_target="Cholesky" | custom-call | tf_op jit(solution)/shard_map/while/body/eval_jaxpr/jit(cholesky)/cholesky | solution.py:232
  418.2 9.8 %custom-call.22 = f32[1,128,128]{1,2,0:T(8,128)S(1)} custom-call(f32[1,128,128]{2,1,0:T(8,128)S(1)} %fusion.440), custom_call_target="InvertDiagBlocksLowerTriangular" | custom-call | tf_op jit(solution)/shard_map/while/body/eval_jaxpr/triangular_solve | solution.py:233
  431.1 11.7 %cholesky.75 = f32[128,128]{1,0:T(8,128)S(1)} custom-call(f32[128,128]{1,0:T(8,128)S(1)} %fusion.439), custom_call_target="Cholesky" | custom-call | tf_op jit(solution)/shard_map/while/body/eval_jaxpr/jit(cholesky)/cholesky | solution.py:232
  444.2 9.8 %custom-call.22 = f32[1,128,128]{1,2,0:T(8,128)S(1)} custom-call(f32[1,128,128]{2,1,0:T(8,128)S(1)} %fusion.440), custom_call_target="InvertDiagBlocksLowerTriangular" | custom-call | tf_op jit(solution)/shard_map/while/body/eval_jaxpr/triangular_solve | solution.py:233
  457.1 11.7 %cholesky.75 = f32[128,128]{1,0:T(8,128)S(1)} custom-call(f32[128,128]{1,0:T(8,128)S(1)} %fusion.439), custom_call_target="Cholesky" | custom-call | tf_op jit(solution)/shard_map/while/body/eval_jaxpr/jit(cholesky)/cholesky | solution.py:232
  470.1 9.8 %custom-call.22 = f32[1,128,128]{1,2,0:T(8,128)S(1)} custom-call(f32[1,128,128]{2,1,0:T(8,128)S(1)} %fusion.440), custom_call_target="InvertDiagBlocksLowerTriangular" | custom-call | tf_op jit(solution)/shard_map/while/body/eval_jaxpr/triangular_solve | solution.py:233
  483.0 11.7 %cholesky.75 = f32[128,128]{1,0:T(8,128)S(1)} custom-call(f32[128,128]{1,0:T(8,128)S(1)} %fusion.439), custom_call_target="Cholesky" | custom-call | tf_op jit(solution)/shard_map/while/body/eval_jaxpr/jit(cholesky)/cholesky | solution.py:232
  496.1 9.8 %custom-call.22 = f32[1,128,128]{1,2,0:T(8,128)S(1)} custom-call(f32[1,128,128]{2,1,0:T(8,128)S(1)} %fusion.440), custom_call_target="InvertDiagBlocksLowerTriangular" | custom-call | tf_op jit(solution)/shard_map/while/body/eval_jaxpr/triangular_solve | solution.py:233
  509.0 11.7 %cholesky.75 = f32[128,128]{1,0:T(8,128)S(1)} custom-call(f32[128,128]{1,0:T(8,128)S(1)} %fusion.439), custom_call_target="Cholesky" | custom-call | tf_op jit(solution)/shard_map/while/body/eval_jaxpr/jit(cholesky)/cholesky | solution.py:232
  522.0 9.8 %custom-call.22 = f32[1,128,128]{1,2,0:T(8,128)S(1)} custom-call(f32[1,128,128]{2,1,0:T(8,128)S(1)} %fusion.440), custom_call_target="InvertDiagBlocksLowerTriangular" | custom-call | tf_op jit(solution)/shard_map/while/body/eval_jaxpr/triangular_solve | solution.py:233
  535.0 11.7 %cholesky.75 = f32[128,128]{1,0:T(8,128)S(1)} custom-call(f32[128,128]{1,0:T(8,128)S(1)} %fusion.439), custom_call_target="Cholesky" | custom-call | tf_op jit(solution)/shard_map/while/body/eval_jaxpr/jit(cholesky)/cholesky | solution.py:232
  548.0 9.8 %custom-call.22 = f32[1,128,128]{1,2,0:T(8,128)S(1)} custom-call(f32[1,128,128]{2,1,0:T(8,128)S(1)} %fusion.440), custom_call_target="InvertDiagBlocksLowerTriangular" | custom-call | tf_op jit(solution)/shard_map/while/body/eval_jaxpr/triangular_solve | solution.py:233
  560.0 33.8 %while.107 = (s32[]{:T(128)}, f32[128]{0:T(128)S(1)}, f32[16,128]{1,0:T(8,128)S(1)}, f32[16,128,128]{2,1,0:T(8,128)}, f32[16,128]{1,0:T(8,128)S(1)}, /*index=5*/f32[16,128,128]{2,1,0:T(8,128)}, s32[]{:T(128)}, s32[]{:T(128)}) while((s32[]{:T(128)}, f32[128]{0:T(128)S(1)}, f32[16,128]{1,0:T(8,128)S(1)}, f32[16,128,128]{2,1,0:T(8,128)}, ...), condition=%wide.region_5.6_spmd, body=%wide.region_4.5_spmd.sunk | while | flops 393346 | bytes 136281 | solution.py:251
  593.9 20.4 %while.108 = (s32[]{:T(128)}, f32[128]{0:T(128)S(1)}, f32[16,128]{1,0:T(8,128)S(1)}, f32[16,128,128]{2,1,0:T(8,128)}, f32[16,128]{1,0:T(8,128)S(1)}, /*index=5*/...) while((s32[]{:T(128)}, f32[128]{0:T(128)S(1)}, f32[16,128]{1,0:T(8,128)S(1)}, ...), condition=%wide.region_7.8_spmd, body=%wide.region_6.7_spmd.sunk | while | flops 393347 | bytes 135793 | solution.py:264
  634.4 13.8 %all_to_all.66 = f32[8,1,1,9]{3,2,1,0:T(1,128)S(1)} all-to-all(f32[8,1,1,9]{3,2,1,0:T(1,128)S(1)} %stack.204), channel_id=1, replica_groups=mesh['axial_0'=8,'axial_1'=2,'circ_0'=4,'circ_1'=4] {'axial_0'}, dimensions={0} | all-to-all | bytes 576 | tf_op jit(solution)/shard_map/all_to_all | solution.py:68
  648.2 8.0 all_to_all.67
  657.7 8.3 all-to-all-start.7
  676.6 33.7 %while.109 = (s32[]{:T(128)}, f32[128]{0:T(128)S(1)}, f32[16,128]{1,0:T(8,128)S(1)}, f32[16,128,128]{2,1,0:T(8,128)}, f32[16,128]{1,0:T(8,128)S(1)}, /*index=5*/f32[16,128,128]{2,1,0:T(8,128)}, s32[]{:T(128)}, s32[]{:T(128)}) while((s32[]{:T(128)}, f32[128]{0:T(128)S(1)}, f32[16,128]{1,0:T(8,128)S(1)}, f32[16,128,128]{2,1,0:T(8,128)}, ...), condition=%wide.region_17.20_spmd, body=%wide.region_16.19_spmd.sunk | while | flops 393346 | bytes 136281 | solution.py:251
  710.4 33.8 %while.110 = (s32[]{:T(128)}, f32[128]{0:T(128)S(1)}, f32[16,128]{1,0:T(8,128)S(1)}, f32[16,128,128]{2,1,0:T(8,128)}, f32[16,128]{1,0:T(8,128)S(1)}, /*index=5*/...) while((s32[]{:T(128)}, f32[128]{0:T(128)S(1)}, f32[16,128]{1,0:T(8,128)S(1)}, ...), condition=%wide.region_19.22_spmd, body=%wide.region_18.21_spmd.sunk | while | flops 393347 | bytes 135793 | solution.py:264
  751.3 15.4 %psum.56 = f32[]{:T(128)} all-reduce(f32[]{:T(128)} %get-tuple-element.757), channel_id=1, replica_groups=mesh['axial_0'=8,'axial_1'=2,'circ_0'=4,'circ_1'=4] {'axial_0'}, use_global_device_ids=true, to_apply=%region_27.30 | all-reduce | flops 1 | bytes 8 | tf_op jit(solution)/shard_map/psum | solution.py:81
  769.8 9.8 %psum.58 = f32[]{:T(128)} all-reduce(f32[]{:T(128)} %psum.57), channel_id=1, replica_groups=mesh['axial_0'=8,'axial_1'=2,'circ_0'=4,'circ_1'=4] {'circ_0'}, use_global_device_ids=true, to_apply=%region_29.32 | all-reduce | flops 1 | bytes 8 | tf_op jit(solution)/shard_map/psum | solution.py:81
  781.3 9.8 %psum.59 = f32[]{:T(128)} all-reduce(f32[]{:T(128)} %psum.58), channel_id=1, replica_groups=mesh['axial_0'=8,'axial_1'=2,'circ_0'=4,'circ_1'=4] {'circ_1'}, use_global_device_ids=true, to_apply=%region_30.33 | all-reduce | flops 1 | bytes 8 | tf_op jit(solution)/shard_map/psum | solution.py:81
  808.4 14.6 %all_to_all.69 = f32[8,1,1,9]{3,2,1,0:T(1,128)S(1)} all-to-all(f32[8,1,1,9]{3,2,1,0:T(1,128)S(1)} %stack.215), channel_id=1, replica_groups=mesh['axial_0'=8,'axial_1'=2,'circ_0'=4,'circ_1'=4] {'axial_0'}, dimensions={0} | all-to-all | bytes 576 | tf_op jit(solution)/shard_map/all_to_all | solution.py:68
  823.0 7.4 all_to_all.70
  831.8 7.7 all-to-all-start.11
  844.3 4.0 all_to_all.71
  851.2 33.8 %while.111 = (s32[]{:T(128)}, f32[128]{0:T(128)S(1)}, f32[16,128]{1,0:T(8,128)S(1)}, f32[16,128,128]{2,1,0:T(8,128)}, f32[16,128]{1,0:T(8,128)S(1)}, /*index=5*/f32[16,128,128]{2,1,0:T(8,128)}, s32[]{:T(128)}, s32[]{:T(128)}) while((s32[]{:T(128)}, f32[128]{0:T(128)S(1)}, f32[16,128]{1,0:T(8,128)S(1)}, f32[16,128,128]{2,1,0:T(8,128)}, ...), condition=%wide.region_34.37_spmd, body=%wide.region_33.36_spmd.sunk | while | flops 393346 | bytes 136281 | solution.py:251
  885.0 33.8 %while.112 = (s32[]{:T(128)}, f32[128]{0:T(128)S(1)}, f32[16,128]{1,0:T(8,128)S(1)}, f32[16,128,128]{2,1,0:T(8,128)}, f32[16,128]{1,0:T(8,128)S(1)}, /*index=5*/...) while((s32[]{:T(128)}, f32[128]{0:T(128)S(1)}, f32[16,128]{1,0:T(8,128)S(1)}, ...), condition=%wide.region_36.39_spmd, body=%wide.region_35.38_spmd.sunk | while | flops 393347 | bytes 135793 | solution.py:264
  925.7 4.2 multiply_reduce_fusion
  929.8 15.3 %psum.60 = f32[]{:T(128)} all-reduce(f32[]{:T(128)} %get-tuple-element.753), channel_id=1, replica_groups=mesh['axial_0'=8,'axial_1'=2,'circ_0'=4,'circ_1'=4] {'axial_0'}, use_global_device_ids=true, to_apply=%region_44.47 | all-reduce | flops 1 | bytes 8 | tf_op jit(solution)/shard_map/psum | solution.py:81
  948.2 9.8 %psum.62 = f32[]{:T(128)} all-reduce(f32[]{:T(128)} %psum.61), channel_id=1, replica_groups=mesh['axial_0'=8,'axial_1'=2,'circ_0'=4,'circ_1'=4] {'circ_0'}, use_global_device_ids=true, to_apply=%region_46.49 | all-reduce | flops 1 | bytes 8 | tf_op jit(solution)/shard_map/psum | solution.py:81
  958.0 9.8 %psum.63 = f32[]{:T(128)} all-reduce(f32[]{:T(128)} %psum.62), channel_id=1, replica_groups=mesh['axial_0'=8,'axial_1'=2,'circ_0'=4,'circ_1'=4] {'circ_1'}, use_global_device_ids=true, to_apply=%region_47.50 | all-reduce | flops 1 | bytes 8 | tf_op jit(solution)/shard_map/psum | solution.py:81
  (865 shorter events, 399.4 us)
Async XLA Ops:
  7.2 23.1 %copy-start.44 = (s32[8,16,256]{2,1,0:T(8,128)S(1)}, s32[8,16,256]{2,1,0:T(8,128)}, u32[]{:S(2)}) copy-start(s32[8,16,256]{2,1,0:T(8,128)} %param.43) | copy-start | bytes 393220
  7.2 23.1 %copy-start.43 = (s32[8,16,256]{2,1,0:T(8,128)S(1)}, s32[8,16,256]{2,1,0:T(8,128)}, u32[]{:S(2)}) copy-start(s32[8,16,256]{2,1,0:T(8,128)} %param.44) | copy-start | bytes 393220
  7.2 20.5 %copy-start.46 = (f32[8,16,256]{2,1,0:T(8,128)S(1)}, f32[8,16,256]{2,1,0:T(8,128)}, u32[]{:S(2)}) copy-start(f32[8,16,256]{2,1,0:T(8,128)} %param.42) | copy-start | bytes 393220
  8.2 11.6 %collective-permute-start = (s32[2,8,1,256]{3,2,1,0:T(1,128)S(1)}, s32[2,8,1,256]{3,2,1,0:T(1,128)S(1)}, u32[]{:S(2)}, u32[]{:S(2)}) collective-permute-start(s32[2,8,1,256]{3,2,1,0:T(1,128)S(1)} %get-tuple-element.842), channel_id=1, source_target_pairs={{0,1},{1,2},{2,3},{3,4},{4,5},{5,6},{6,7},{7,8},{8,9},{9,10},{10,1... | collective-permute-start | bytes 49160 | tf_op jit(solution)/shard_map/ppermute | solution.py:42
  9.9 10.0 %collective-permute-start.1 = (s32[2,8,1,256]{3,2,1,0:T(1,128)S(1)}, s32[2,8,1,256]{3,2,1,0:T(1,128)S(1)}, u32[]{:S(2)}, u32[]{:S(2)}) collective-permute-start(s32[2,8,1,256]{3,2,1,0:T(1,128)S(1)} %get-tuple-element.843), channel_id=1, source_target_pairs={{1,0},{2,1},{3,2},{4,3},{5,4},{6,5},{7,6},{8,7},{9,8},{10,9},{11,1... | collective-permute-start | bytes 49160 | tf_op jit(solution)/shard_map/ppermute | solution.py:43
  11.2 4.3 collective-permute-start.4
  12.9 3.7 collective-permute-start.5
  15.1 31.9 %copy-start.40 = (pred[8,8,16,256]{3,0,1,2:T(8,128)(4,1)}, pred[8,8,16,256]{3,0,1,2:T(8,128)(4,1)S(1)}, u32[]{:S(2)}) copy-start(pred[8,8,16,256]{3,0,1,2:T(8,128)(4,1)S(1)} %iota_compare_fusion.6) | copy-start | bytes 786436
  15.1 15.2 %copy-start.52 = (f32[16,13,1,1]{0,1,3,2:T(8,128)S(1)}, f32[16,13,1,1]{0,1,3,2:T(8,128)}, u32[]{:S(2)}) copy-start(f32[16,13,1,1]{0,1,3,2:T(8,128)} %constant.1450) | copy-start | bytes 2500
  17.3 10.4 %collective-permute-start.6 = (f32[1,18,256]{2,1,0:T(8,128)S(1)}, f32[1,18,256]{2,1,0:T(8,128)S(1)}, u32[]{:S(2)}, u32[]{:S(2)}) collective-permute-start(f32[1,18,256]{2,1,0:T(8,128)S(1)} %get-tuple-element.948), channel_id=1, source_target_pairs={{0,16},{16,32},{32,48},{48,64},{64,80},{80,96},{96,112},{112,128},... | collective-permute-start | bytes 55304 | tf_op jit(solution)/shard_map/ppermute | solution.py:42
  18.6 9.1 collective-permute-start.7
  20.7 7.1 collective-permute-start.2
  25.9 4.4 collective-permute-start.3
  37.1 1.1 copy-start.31
  37.1 1.2 copy-start.27
  37.1 1.4 copy-start.16
  37.1 1.5 copy-start.10
  37.1 1.6 copy-start.8
  37.1 1.7 copy-start.2
  37.1 1.9 copy-start
  37.1 2.0 copy-start.18
  37.1 2.1 copy-start.35
  37.2 2.3 copy-start.23
  37.2 2.5 copy-start.20
  37.2 2.7 copy-start.14
  37.2 2.9 copy-start.12
  37.2 3.1 copy-start.6
  37.2 3.3 copy-start.4
  69.3 17.5 %all-to-all-start = ((f32[16,1,384]{2,1,0:T(1,128)}), f32[16,1,384]{2,1,0:T(1,128)S(1)}, u32[]{:S(2)}, u32[]{:S(2)}) async-start(f32[16,1,384]{2,1,0:T(1,128)} %reshape.1223), calls=%async_computation | async-start | bytes 49152 | tf_op jit(solution)/shard_map/all_to_all | solution.py:50
  81.4 59.0 %all-gather.2.cloned.1.call-start = ((), (), s32[]{:S(2)}) async-start(), calls=%async_computation.13 | async-start | bytes 2228224 | tf_op jit(solution)/shard_map/all_gather | solution.py:313
  92.0 16.2 %copy-start.54 = (s32[10]{0:T(128)S(1)}, s32[10]{0:T(128)}, u32[]{:S(2)}) copy-start(s32[10]{0:T(128)} %constant.1444) | copy-start | bytes 124
  92.1 16.2 %copy-start.53 = (s32[18]{0:T(128)S(1)}, s32[18]{0:T(128)}, u32[]{:S(2)}) copy-start(s32[18]{0:T(128)} %constant.1445) | copy-start | bytes 220
  96.6 19.4 %all-to-all-start.1 = ((f32[8,1,1,9]{3,2,1,0:T(1,128)}), f32[8,1,1,9]{3,2,1,0:T(1,128)S(1)}, u32[]{:S(2)}, u32[]{:S(2)}) async-start(f32[8,1,1,9]{3,2,1,0:T(1,128)} %stack.193), calls=%async_computation.1 | async-start | bytes 8192 | tf_op jit(solution)/shard_map/all_to_all | solution.py:68
  116.6 8.6 all-to-all-start.2
  126.6 8.5 all-to-all-start.3
  593.9 22.3 %copy-start.50 = (pred[8,10,18,256]{3,0,1,2:T(8,128)(4,1)S(1)}, pred[8,10,18,256]{3,0,1,2:T(8,128)(4,1)}, u32[]{:S(2)}) copy-start(pred[8,10,18,256]{3,0,1,2:T(8,128)(4,1)} %iota_compare_fusion.5) | copy-start | bytes 1105924
  614.3 1.9 copy-start.39
  617.2 1.1 copy-start.9
  617.2 1.2 copy-start.11
  617.2 1.2 copy-start.13
  617.2 1.2 copy-start.15
  617.2 1.3 copy-start.17
  617.2 1.3 copy-start.19
  617.2 1.3 copy-start.21
  617.2 1.4 copy-start.24
  617.2 1.4 copy-start.28
  617.3 1.4 copy-start.32
  617.3 1.4 copy-start.36
  617.3 1.5 copy-start.51
  620.5 3.7 collective-permute-start.8
  622.0 3.7 collective-permute-start.9
  625.7 4.7 collective-permute-start.10
  627.0 3.9 collective-permute-start.11
  632.4 1.2 copy-start.48
  657.7 12.1 %all-to-all-start.7 = ((f32[4,1,288]{2,1,0:T(1,128)}), f32[4,1,288]{2,1,0:T(1,128)S(1)}, u32[]{:S(2)}, u32[]{:S(2)}) async-start(f32[4,1,288]{2,1,0:T(1,128)} %reshape.1227), calls=%async_computation.7 | async-start | bytes 12288 | tf_op jit(solution)/shard_map/all_to_all | solution.py:68
  676.5 68.2 %copy-start.45 = (f32[8,2,4,4,1,9]{5,3,2,1,0,4:T(4,128)}, f32[8,2,4,4,1,9]{5,3,2,1,0,4:T(4,128)S(1)}, u32[]{:S(2)}) copy-start(f32[8,2,4,4,1,9]{5,3,2,1,0,4:T(4,128)S(1)} %copy.445) | copy-start | bytes 27652
  748.0 1.1 copy-start.49
  794.1 3.7 collective-permute-start.12
  795.3 3.7 collective-permute-start.13
  799.0 4.5 collective-permute-start.14
  800.3 3.9 collective-permute-start.15
  804.3 1.1 copy-start.38
  806.4 1.2 copy-start.47
  831.8 11.5 %all-to-all-start.11 = ((f32[4,1,288]{2,1,0:T(1,128)}), f32[4,1,288]{2,1,0:T(1,128)S(1)}, u32[]{:S(2)}, u32[]{:S(2)}) async-start(f32[4,1,288]{2,1,0:T(1,128)} %reshape.1229), calls=%async_computation.11 | async-start | bytes 12288 | tf_op jit(solution)/shard_map/all_to_all | solution.py:68
  (14 other events, 14.0 us)
Sparse Core Ops, SparseCore 0:
  93.8 43.6 all-gather.1
